TPU v7x, 32 devices: a whole 2x2x4 slice. The times are simulated.
32 devices in a mesh: seq: 8 (over y, x, core), fsdp: 4 (over z).
Axes of the slice: x: 2, y: 2, z: 4, core: 2. Of those that a mesh axis runs over, the one named last changes fastest.
Arguments:
- queries: bfloat16 [4, 2048, 4096], P('fsdp', 'seq'), may hold values from -1000 to 1000
- keys: bfloat16 [4, 2048, 4096], P('fsdp', 'seq'), may hold values from -1000 to 1000
- values: bfloat16 [4, 2048, 4096], P('fsdp', 'seq'), may hold values from -24 to 24
- targets: bfloat16 [4, 2048, 4096], P('fsdp', 'seq'), may hold values from -2.390625 to 2.390625
- tile_lists: int32 [4, 128, 12], P('fsdp', 'seq'), may hold values from 0 to 127, as said below
- query_gain: float32 [4096], P('fsdp'), may hold values from 0.1 to 1.9
- key_gain: float32 [4096], P('fsdp'), may hold values from 0.1 to 1.9
Outputs:
- grad_queries: bfloat16 [4, 2048, 4096], P('fsdp', 'seq')
- grad_keys: bfloat16 [4, 2048, 4096], P('fsdp', 'seq')
- grad_values: bfloat16 [4, 2048, 4096], P('fsdp', 'seq')
- grad_query_gain: float32 [4096], P('fsdp')
- grad_key_gain: float32 [4096], P('fsdp')
Inputs may be any that keep to these rules, and one draw needn't show every extreme that they name: `tile_lists`: tiles are numbered frame by frame and, inside a frame of 4 by 4 tiles, row by row. Entry 0 of each list is the query tile itself; every entry names a tile at most one frame, one tile row and one tile column away from the query tile; entries may repeat.
All inputs are finite; a program needn't handle non-finite values.
Results may differ from a plain program's by a relative error of at most 0.022.
The roundings to bfloat16 on the way count: a program that leaves them out, or rounds other values in their place, can miss the bound.
Values may be sent and summed in bfloat16 or wider, within the bound.
A program may use at most 192 MiB of HBM per device.

v0:
```python
import math

import jax
import jax.numpy as jnp
from jax import lax
from jax.experimental import pallas as pl
from jax.sharding import PartitionSpec as P


HD = 128
TILE = 16
EPS = 1e-06
CHUNKS = 2
STEP_HEADS = 4


def norm_forward(matrix, scaling):
    widened = matrix.astype(jnp.float32)
    spread = jnp.sqrt(jnp.mean(widened * widened, axis=-1, keepdims=True) + EPS)
    return (widened / spread * scaling).astype(jnp.bfloat16), spread


def norm_backward(returned, matrix, spread, scaling):
    unit_rows = matrix.astype(jnp.float32) / spread
    upstream = returned * scaling
    projected = jnp.mean(upstream * unit_rows, axis=-1, keepdims=True)
    grad_matrix = ((upstream - unit_rows * projected) / spread).astype(jnp.bfloat16)
    return grad_matrix, jnp.sum(returned * unit_rows, axis=0)


def contract(a, b, dim_a, dim_b):
    return lax.dot_general(
        a, b, (((dim_a,), (dim_b,)), ((), ())), preferred_element_type=jnp.float32
    )


def attend_kernel(
    bias, q, kl, ko, kr, vl, vo, vr, t, dq, dkl, dko, dkr, dvl, dvo, dvr
):
    rows = q.shape[0]
    factor = 1.0 / math.sqrt(HD)
    for h in range(q.shape[1] // HD):
        at = slice(h * HD, (h + 1) * HD)
        query = q[:, at]
        key = jnp.concatenate([kl[:, at], ko[:, at], kr[:, at]], axis=0)
        value = jnp.concatenate([vl[:, at], vo[:, at], vr[:, at]], axis=0)
        scores = contract(key, query, 1, 1) * factor + bias[...]
        weights = jnp.exp(scores - jnp.max(scores, axis=0, keepdims=True))
        shares = weights * (1.0 / jnp.sum(weights, axis=0, keepdims=True))
        shares_low = shares.astype(jnp.bfloat16)
        attended = contract(value, shares_low, 0, 0)
        wanted = t[:, at].astype(jnp.float32).T
        residual_low = (attended - wanted).astype(jnp.bfloat16)
        residual_wide = residual_low.astype(jnp.float32)
        delta = jnp.sum(residual_wide * attended, axis=0, keepdims=True)
        dvalue = contract(shares_low, residual_low, 1, 1).astype(jnp.bfloat16)
        dshares = contract(value, residual_low, 1, 0)
        dscores_low = (shares * (dshares - delta) * factor).astype(jnp.bfloat16)
        dkey = contract(dscores_low, query, 1, 0).astype(jnp.bfloat16)
        dq[:, at] = contract(key, dscores_low, 0, 0).T.astype(jnp.bfloat16)
        dkl[:, at], dko[:, at], dkr[:, at] = (
            dkey[:rows],
            dkey[rows : 2 * rows],
            dkey[2 * rows :],
        )
        dvl[:, at], dvo[:, at], dvr[:, at] = (
            dvalue[:rows],
            dvalue[rows : 2 * rows],
            dvalue[2 * rows :],
        )


def attend(chunk, width, bias, q, kl, ko, kr, vl, vo, vr, t):
    rows = q.shape[0]
    block = min(STEP_HEADS * HD, width)
    steps = width // block
    heads = width // HD
    whole = pl.BlockSpec((rows, block), lambda i: (0, chunk * steps + i))
    part = pl.BlockSpec((rows, block), lambda i: (0, i))
    fixed = pl.BlockSpec(bias.shape, lambda i: (0, 0))
    out = jax.ShapeDtypeStruct((rows, width), jnp.bfloat16)
    return pl.pallas_call(
        attend_kernel,
        grid=(steps,),
        in_specs=[fixed, whole, part, whole, part, part, whole, part, whole],
        out_specs=[part] * 7,
        out_shape=[out] * 7,
        cost_estimate=pl.CostEstimate(
            flops=5 * 2 * rows * 3 * rows * HD * heads * 3,
            bytes_accessed=15 * rows * width * 2,
            transcendentals=3 * rows * rows * heads,
        ),
    )(bias, q, kl, ko, kr, vl, vo, vr, t)


def gather_gains(part):
    count, me = lax.axis_size("fsdp"), lax.axis_index("fsdp")
    pieces = [part] + [
        lax.ppermute(part, "fsdp", [(i, (i + s) % count) for i in range(count)])
        for s in range(1, count)
    ]
    blocks = []
    for j in range(count):
        block = pieces[0]
        for s in range(1, count):
            block = jnp.where((me - s - j) % count == 0, pieces[s], block)
        blocks.append(block)
    return jnp.concatenate(blocks, axis=1)


def sum_gains(parts):
    count, me = lax.axis_size("fsdp"), lax.axis_index("fsdp")
    blocks = parts.reshape(parts.shape[0], count, -1)
    total = lax.dynamic_index_in_dim(blocks, me, axis=1, keepdims=False)
    for s in range(1, count):
        there = lax.dynamic_index_in_dim(blocks, (me + s) % count, axis=1, keepdims=False)
        total = total + lax.ppermute(there, "fsdp", [(i, (i + s) % count) for i in range(count)])
    frame_count = lax.axis_size("seq")
    if frame_count & (frame_count - 1):
        return lax.psum(total, "seq")
    step = 1
    while step < frame_count:
        total = total + lax.ppermute(total, "seq", [(i, i ^ step) for i in range(frame_count)])
        step *= 2
    return total


def shards(queries, keys, values, targets, tile_lists, query_gain, key_gain):
    q, k, v, t = queries[0], keys[0], values[0], targets[0]
    rows, features = q.shape
    frame_count = lax.axis_size("seq")
    frame = lax.axis_index("seq")
    rightward = [(i, i + 1) for i in range(frame_count - 1)]
    leftward = [(i + 1, i) for i in range(frame_count - 1)]
    to_right = lambda x: lax.ppermute(x, "seq", rightward)
    to_left = lambda x: lax.ppermute(x, "seq", leftward)

    middle = frame_count // 2
    near = lambda pairs: [p for p in pairs if set(p) != {middle - 1, middle}]
    near_right = lambda x: lax.ppermute(x, "seq", near(rightward))
    near_left = lambda x: lax.ppermute(x, "seq", near(leftward))

    def relay(x):
        out = lax.ppermute(x, "seq", [(middle - 1, frame_count - 1), (middle, 0)])
        return lax.ppermute(out, "seq", [(frame_count - 1, middle), (0, middle - 1)])

    v_far = relay(v)
    gains = gather_gains(jnp.stack([query_gain, key_gain]))
    query_scale, key_scale = gains[0], gains[1]
    key_norm, key_rms = norm_forward(k, key_scale)
    query_norm, query_rms = norm_forward(q, query_scale)

    tiles = rows // TILE
    lists = jnp.repeat(tile_lists[0], TILE, axis=0).T
    labels = (frame - 1) * tiles + jnp.arange(3 * rows, dtype=jnp.int32) // TILE
    labels = jnp.where((labels >= 0) & (labels < frame_count * tiles), labels, -1)[:, None]
    allowed = lists[0:1] == labels
    for slot in range(1, lists.shape[0]):
        allowed = allowed | (lists[slot : slot + 1] == labels)
    bias = jnp.where(allowed, 0.0, -jnp.inf).astype(jnp.float32)

    width = features // CHUNKS
    held = []
    before = None
    for c in range(CHUNKS):
        at = slice(c * width, (c + 1) * width)
        v_part, k_part = v[:, at], key_norm[:, at]
        if before is not None:
            v_part, _ = lax.optimization_barrier((v_part, before[0]))
            k_part, _ = lax.optimization_barrier((k_part, before[1]))
        vl, vr = near_right(v_part), near_left(v_part)
        kl, kr = to_right(k_part), to_left(k_part)
        before = (vl, kl)
        held.append((kl, kr, vl, vr))

    dq, dk, dv = [], [], []
    for c in range(CHUNKS):
        kl, kr, vl, vr = held[c]
        far = v_far
        if c > 0:
            vl, vr, far, _ = lax.optimization_barrier((vl, vr, v_far, dq_c))
        far = far[:, c * width : (c + 1) * width]
        vl = jnp.where(frame == middle, far, vl)
        vr = jnp.where(frame == middle - 1, far, vr)
        dq_c, dkl, dko, dkr, dvl, dvo, dvr = attend(
            c, width, bias, query_norm, kl, key_norm, kr, vl, v, vr, t
        )
        dq.append(dq_c.astype(jnp.float32))
        if c == 0:
            far = relay(
                jnp.concatenate(
                    [jnp.where(frame == middle, dkl, dkr), jnp.where(frame == middle, dvl, dvr)]
                ),
            )
            k_terms = (dko, near_left(dkl), near_right(dkr), far[:rows])
            v_terms = (dvo, near_left(dvl), near_right(dvr), far[rows:])
        else:
            k_terms = (dko, to_left(dkl), to_right(dkr))
            v_terms = (dvo, to_left(dvl), to_right(dvr))
        wide = lambda terms: sum(x.astype(jnp.float32) for x in terms).astype(jnp.bfloat16)
        dk.append(wide(k_terms).astype(jnp.float32))
        dv.append(wide(v_terms))

    grad_q, q_gain = norm_backward(jnp.concatenate(dq, axis=1), q, query_rms, query_scale)
    grad_k, k_gain = norm_backward(jnp.concatenate(dk, axis=1), k, key_rms, key_scale)
    gain_grads = sum_gains(jnp.stack([q_gain, k_gain]))
    return (
        grad_q[None],
        grad_k[None],
        jnp.concatenate(dv, axis=1)[None],
        gain_grads[0],
        gain_grads[1],
    )


def solution(mesh):
    rows = P("fsdp", "seq", None)
    return jax.shard_map(
        shards,
        mesh=mesh,
        in_specs=(rows, rows, rows, rows, rows, P("fsdp"), P("fsdp")),
        out_specs=(rows, rows, rows, P("fsdp"), P("fsdp")),
        check_vma=False,
    )
```

profile of v0, /device:TPU:0, one launch (start us, length us, event | category | flops | bytes accessed | tf_op | source)
XLA Modules:
  0.0 225.0 jit_solution(14855198920916561904)
XLA Ops:
  1.4 5.1 %collective-permute-start = (f32[2,1024]{1,0:T(2,128)S(1)}, f32[2,1024]{1,0:T(2,128)S(1)}, u32[]{:S(2)}, u32[]{:S(2)}) collective-permute-start(f32[2,1024]{1,0:T(2,128)S(1)} %pad_maximum_fusion.4), channel_id=1, source_target_pairs={{0,3},{1,0},{2,1},{3,2},{4,7},{5,4},{6,5},{7,6},{8,11},{9,8},{10,9... | collective-permute-start | bytes 24584 | tf_op jit(solution)/shard_map/ppermute | solution.py:99
  7.5 1.4 collective-permute-start.5
  8.9 2.7 %fusion.26 = (bf16[256,2048]{1,0:T(8,128)(2,1)}, bf16[256,2048]{1,0:T(8,128)(2,1)S(1)}) fusion(bf16[256,4096]{1,0:T(8,128)(2,1)} %bitcast.80), kind=kLoop, calls=%fused_computation.80 | loop fusion | bytes 4194304 | tf_op jit(solution)/shard_map/slice | solution.py:167
  11.7 2.6 %collective-permute-start.7 = (bf16[256,2048]{1,0:T(8,128)(2,1)}, bf16[256,2048]{1,0:T(8,128)(2,1)}, u32[]{:S(2)}, u32[]{:S(2)}) collective-permute-start(bf16[256,2048]{1,0:T(8,128)(2,1)} %get-tuple-element.53), channel_id=1, source_target_pairs={{0,4},{4,8},{8,12},{16,20},{20,24},{24,28},{1,5},{5,9},{9,13},{17,... | collective-permute-start | bytes 3145736 | tf_op jit(solution)/shard_map/ppermute | solution.py:140
  16.6 2.1 or_select_fusion.bias
  18.7 1.3 collective-permute-start.8
  20.1 15.8 %collective-permute-done.5 = bf16[256,4096]{1,0:T(8,128)(2,1)} collective-permute-done((bf16[256,4096]{1,0:T(8,128)(2,1)}, bf16[256,4096]{1,0:T(8,128)(2,1)}, u32[]{:S(2)}, u32[]{:S(2)}) %collective-permute-start.5) | collective-permute-done | bytes 2097184 | tf_op jit(solution)/shard_map/ppermute | solution.py:144
  35.9 2.6 %collective-permute-start.6 = (bf16[256,4096]{1,0:T(8,128)(2,1)}, bf16[256,4096]{1,0:T(8,128)(2,1)}, u32[]{:S(2)}, u32[]{:S(2)}) collective-permute-start(bf16[256,4096]{1,0:T(8,128)(2,1)} %collective-permute-done.5), channel_id=1, source_target_pairs={{28,16},{0,12},{29,17},{1,13},{30,18},{2,14},{31,19},{3,15}} | collective-permute-start | bytes 6291464 | tf_op jit(solution)/shard_map/ppermute | solution.py:145
  38.5 2.2 multiply_convert_fusion.ko
  40.7 1.6 fusion.27
  42.7 2.3 %collective-permute-start.3 = (bf16[256,2048]{1,0:T(8,128)(2,1)}, bf16[256,2048]{1,0:T(8,128)(2,1)}, u32[]{:S(2)}, u32[]{:S(2)}) collective-permute-start(bf16[256,2048]{1,0:T(8,128)(2,1)} %get-tuple-element.55), channel_id=1, source_target_pairs={{0,4},{4,8},{8,12},{12,16},{16,20},{20,24},{24,28},{1,5},{5,9},{9,... | collective-permute-start | bytes 3145736 | tf_op jit(solution)/shard_map/ppermute | solution.py:135
  45.0 1.3 collective-permute-start.4
  46.3 2.0 multiply_convert_fusion.1.q
  48.3 4.0 %collective-permute-start.11 = (bf16[256,2048]{1,0:T(8,128)(2,1)S(1)}, bf16[256,2048]{1,0:T(8,128)(2,1)}, u32[]{:S(2)}, u32[]{:S(2)}) collective-permute-start(bf16[256,2048]{1,0:T(8,128)(2,1)S(1)} %get-tuple-element.26), channel_id=1, source_target_pairs={{0,4},{4,8},{8,12},{16,20},{20,24},{24,28},{1,5},{5,9},{9,13},{17,... | collective-permute-start | bytes 3145736 | tf_op jit(solution)/shard_map/ppermute | solution.py:140
  52.3 1.3 collective-permute-start.12
  53.6 4.0 %collective-permute-start.9 = (bf16[256,2048]{1,0:T(8,128)(2,1)}, bf16[256,2048]{1,0:T(8,128)(2,1)}, u32[]{:S(2)}, u32[]{:S(2)}) collective-permute-start(bf16[256,2048]{1,0:T(8,128)(2,1)} %get-tuple-element.25), channel_id=1, source_target_pairs={{0,4},{4,8},{8,12},{12,16},{16,20},{20,24},{24,28},{1,5},{5,9},{9,... | collective-permute-start | bytes 3145736 | tf_op jit(solution)/shard_map/ppermute | solution.py:135
  57.6 23.9 %collective-permute-done.6 = bf16[256,4096]{1,0:T(8,128)(2,1)} collective-permute-done((bf16[256,4096]{1,0:T(8,128)(2,1)}, bf16[256,4096]{1,0:T(8,128)(2,1)}, u32[]{:S(2)}, u32[]{:S(2)}) %collective-permute-start.6) | collective-permute-done | bytes 2097184 | tf_op jit(solution)/shard_map/ppermute | solution.py:145
  81.5 1.3 collective-permute-start.10
  82.8 3.3 %broadcast_select_fusion.1 = (bf16[256,2048]{1,0:T(8,128)(2,1)}, bf16[256,2048]{1,0:T(8,128)(2,1)}) fusion(bf16[256,2048]{1,0:T(8,128)(2,1)} %collective-permute-done.8, pred[]{:T(512)S(6)} %eq.252, bf16[256,4096]{1,0:T(8,128)(2,1)} %collective-permute-done.6, bf16[256,2048]{1,0:T(8,128)(2,1)} %collective-permute-done.7, pred[]{:T(512)S(6)} %eq.251), kind=kLoop, calls=%fused_computation.37 | loop fusion | flops 1048576 | bytes 5242882 | tf_op jit(solution)/shard_map/jit(_where)/select_n | solution.py:184
  86.1 22.3 %shard_map.110 = (bf16[256,2048]{1,0:T(8,128)(2,1)}, bf16[256,2048]{1,0:T(8,128)(2,1)}, bf16[256,2048]{1,0:T(8,128)(2,1)}, bf16[256,2048]{1,0:T(8,128)(2,1)}, bf...) custom-call(f32[768,256]{1,0:T(8,128)} %or_select_fusion.bias, ...), custom_call_target="tpu_custom_call" | custom-call | flops 12079595520 | bytes 15728640 | tf_op jit(solution)/shard_map/pallas_call | solution.py:82
  108.5 4.0 %collective-permute-start.20 = (bf16[256,2048]{1,0:T(8,128)(2,1)}, bf16[256,2048]{1,0:T(8,128)(2,1)}, u32[]{:S(2)}, u32[]{:S(2)}) collective-permute-start(bf16[256,2048]{1,0:T(8,128)(2,1)} %get-tuple-element.35), channel_id=1, source_target_pairs={{0,4},{4,8},{8,12},{16,20},{20,24},{24,28},{1,5},{5,9},{9,13},{17,... | collective-permute-start | bytes 3145736 | tf_op jit(solution)/shard_map/ppermute | solution.py:140
  112.5 1.7 broadcast_select_fusion.2
  114.2 1.3 collective-permute-start.19
  115.5 1.6 pad_maximum_fusion.2
  117.1 1.5 collective-permute-start.15
  118.6 3.4 %broadcast_select_fusion = (bf16[256,2048]{1,0:T(8,128)(2,1)}, bf16[256,2048]{1,0:T(8,128)(2,1)}) fusion(bf16[256,2048]{1,0:T(8,128)(2,1)} %collective-permute-done.12, pred[]{:T(512)S(6)} %eq.252, bf16[256,4096]{1,0:T(8,128)(2,1)} %collective-permute-done.6, bf16[256,2048]{1,0:T(8,128)(2,1)} %collective-permute-done.11, pred[]{:T(512)S(6)} %eq.251), kind=kLoop, calls=%fused_computation.36 | loop fusion | flops 1048576 | bytes 5242882 | tf_op jit(solution)/shard_map/jit(_where)/select_n | solution.py:184
  122.0 22.5 %shard_map.111 = (bf16[256,2048]{1,0:T(8,128)(2,1)}, bf16[256,2048]{1,0:T(8,128)(2,1)}, bf16[256,2048]{1,0:T(8,128)(2,1)}, bf16[256,2048]{1,0:T(8,128)(2,1)}, bf...) custom-call(f32[768,256]{1,0:T(8,128)} %or_select_fusion.bias, ...), custom_call_target="tpu_custom_call" | custom-call | flops 12079595520 | bytes 15728640 | tf_op jit(solution)/shard_map/pallas_call | solution.py:82
  144.5 4.5 %collective-permute-start.18 = (bf16[256,2048]{1,0:T(8,128)(2,1)}, bf16[256,2048]{1,0:T(8,128)(2,1)}, u32[]{:S(2)}, u32[]{:S(2)}) collective-permute-start(bf16[256,2048]{1,0:T(8,128)(2,1)} %get-tuple-element.38), channel_id=1, source_target_pairs={{0,4},{4,8},{8,12},{12,16},{16,20},{20,24},{24,28},{1,5},{5,9},{9,... | collective-permute-start | bytes 3145736 | tf_op jit(solution)/shard_map/ppermute | solution.py:135
  149.0 1.4 collective-permute-start.17
  151.3 6.0 %collective-permute-start.16 = (bf16[512,2048]{1,0:T(8,128)(2,1)}, bf16[512,2048]{1,0:T(8,128)(2,1)}, u32[]{:S(2)}, u32[]{:S(2)}) collective-permute-start(bf16[512,2048]{1,0:T(8,128)(2,1)} %collective-permute-done.15), channel_id=1, source_target_pairs={{28,16},{0,12},{29,17},{1,13},{30,18},{2,14},{31,19},{3,15}} | collective-permute-start | bytes 6291464 | tf_op jit(solution)/shard_map/ppermute | solution.py:145
  157.3 1.7 multiply_reduce_fusion.1
  159.0 7.7 %collective-permute-start.14 = (bf16[256,2048]{1,0:T(8,128)(2,1)}, bf16[256,2048]{1,0:T(8,128)(2,1)}, u32[]{:S(2)}, u32[]{:S(2)}) collective-permute-start(bf16[256,2048]{1,0:T(8,128)(2,1)} %get-tuple-element.33), channel_id=1, source_target_pairs={{0,4},{4,8},{8,12},{16,20},{20,24},{24,28},{1,5},{5,9},{9,13},{17,... | collective-permute-start | bytes 3145736 | tf_op jit(solution)/shard_map/ppermute | solution.py:140
  166.7 1.3 collective-permute-start.13
  168.0 2.2 fusion.13
  170.2 2.5 %fusion.15 = f32[256,2048]{1,0:T(8,128)S(1)} fusion(bf16[256,2048]{1,0:T(8,128)(2,1)} %collective-permute-done.18, bf16[256,2048]{1,0:T(8,128)(2,1)} %collective-permute-done.17, bf16[256,2048]{1,0:T(8,128)(2,1)} %get-tuple-element.36), kind=kLoop, calls=%fused_computation.35 | loop fusion | flops 3670016 | bytes 5242880 | tf_op jit(solution)/shard_map/convert_element_type | solution.py:201
  172.8 11.8 %collective-permute-start.22 = (bf16[256,2048]{1,0:T(8,128)(2,1)}, bf16[256,2048]{1,0:T(8,128)(2,1)}, u32[]{:S(2)}, u32[]{:S(2)}) collective-permute-start(bf16[256,2048]{1,0:T(8,128)(2,1)} %get-tuple-element.42), channel_id=1, source_target_pairs={{0,4},{4,8},{8,12},{12,16},{16,20},{20,24},{24,28},{1,5},{5,9},{9,... | collective-permute-start | bytes 3145736 | tf_op jit(solution)/shard_map/ppermute | solution.py:135
  184.5 1.3 collective-permute-start.21
  185.9 11.2 %collective-permute-done.16 = bf16[512,2048]{1,0:T(8,128)(2,1)} collective-permute-done((bf16[512,2048]{1,0:T(8,128)(2,1)}, bf16[512,2048]{1,0:T(8,128)(2,1)}, u32[]{:S(2)}, u32[]{:S(2)}) %collective-permute-start.16) | collective-permute-done | bytes 2097184 | tf_op jit(solution)/shard_map/ppermute | solution.py:145
  197.0 4.6 %add_convert_fusion.1 = (bf16[256,2048]{1,0:T(8,128)(2,1)S(1)}, f32[256,2048]{1,0:T(8,128)S(1)}) fusion(bf16[256,2048]{1,0:T(8,128)(2,1)} %collective-permute-done.20, bf16[256,2048]{1,0:T(8,128)(2,1)} %collective-permute-done.19, bf16[256,2048]{1,0:T(8,128)(2,1)S(1)} %copy-done.12, bf16[512,2048]{1,0:T(8,128)(2,1)} %collective-permute-done.16, ...), kind=kLoop, calls=%fused_computation.31 | loop fusion | flops 8912896 | bytes 11534336 | tf_op jit(solution)/shard_map/convert_element_type | solution.py:200
  201.7 1.7 multiply_reduce_fusion
  203.5 2.9 %collective-permute-start.25 = (f32[2,1024]{1,0:T(2,128)S(1)}, f32[2,1024]{1,0:T(2,128)S(1)}, u32[]{:S(2)}, u32[]{:S(2)}) collective-permute-start(f32[2,1024]{1,0:T(2,128)S(1)} %bitcast.95), channel_id=1, source_target_pairs={{0,3},{1,0},{2,1},{3,2},{4,7},{5,4},{6,5},{7,6},{8,11},{9,8},{10,9... | collective-permute-start | bytes 24584 | tf_op jit(solution)/shard_map/ppermute | solution.py:117
  207.6 2.5 %add_convert_fusion = bf16[256,2048]{1,0:T(8,128)(2,1)S(1)} fusion(bf16[256,2048]{1,0:T(8,128)(2,1)} %collective-permute-done.22, bf16[256,2048]{1,0:T(8,128)(2,1)} %collective-permute-done.21, bf16[256,2048]{1,0:T(8,128)(2,1)} %get-tuple-element.40), kind=kLoop, calls=%fused_computation.30 | loop fusion | flops 3145728 | bytes 4194304 | tf_op jit(solution)/shard_map/convert_element_type | solution.py:200
  210.9 2.0 collective-permute-done.23
  212.9 3.3 %collective-permute-start.26 = (f32[2,1024]{1,0:T(2,128)S(1)}, f32[2,1024]{1,0:T(2,128)S(1)}, u32[]{:S(2)}, u32[]{:S(2)}) collective-permute-start(f32[2,1024]{1,0:T(2,128)S(1)} %fusion.17), channel_id=1, source_target_pairs={{0,4},{4,0},{8,12},{12,8},{16,20},{20,16},{24,28},{28,24},{1,5},{5... | collective-permute-start | bytes 24584 | tf_op jit(solution)/shard_map/ppermute | solution.py:123
  217.2 2.2 fusion.12
  219.3 1.4 collective-permute-done.27
  221.1 1.5 maximum_bitcast_fusion
  222.6 1.8 collective-permute-done.28
  (91 shorter events, 9.4 us)
Async XLA Ops:
  1.4 17.3 %collective-permute-start = (f32[2,1024]{1,0:T(2,128)S(1)}, f32[2,1024]{1,0:T(2,128)S(1)}, u32[]{:S(2)}, u32[]{:S(2)}) collective-permute-start(f32[2,1024]{1,0:T(2,128)S(1)} %pad_maximum_fusion.4), channel_id=1, source_target_pairs={{0,3},{1,0},{2,1},{3,2},{4,7},{5,4},{6,5},{7,6},{8,11},{9,8},{10,9... | collective-permute-start | bytes 24584 | tf_op jit(solution)/shard_map/ppermute | solution.py:99
  6.5 13.5 %collective-permute-start.1 = (f32[2,1024]{1,0:T(2,128)S(1)}, f32[2,1024]{1,0:T(2,128)S(1)}, u32[]{:S(2)}, u32[]{:S(2)}) collective-permute-start(f32[2,1024]{1,0:T(2,128)S(1)} %pad_maximum_fusion.4), channel_id=1, source_target_pairs={{0,2},{1,3},{2,0},{3,1},{4,6},{5,7},{6,4},{7,5},{8,10},{9,11},{10,... | collective-permute-start | bytes 24584 | tf_op jit(solution)/shard_map/ppermute | solution.py:99
  6.5 13.5 %collective-permute-start.2 = (f32[2,1024]{1,0:T(2,128)S(1)}, f32[2,1024]{1,0:T(2,128)S(1)}, u32[]{:S(2)}, u32[]{:S(2)}) collective-permute-start(f32[2,1024]{1,0:T(2,128)S(1)} %pad_maximum_fusion.4), channel_id=1, source_target_pairs={{0,1},{1,2},{2,3},{3,0},{4,5},{5,6},{6,7},{7,4},{8,9},{9,10},{10,1... | collective-permute-start | bytes 24584 | tf_op jit(solution)/shard_map/ppermute | solution.py:99
  7.5 6.7 %copy-start.15 = (s32[1,16,12]{1,0,2:T(1,128)S(1)}, s32[1,16,12]{1,0,2:T(1,128)}, u32[]{:S(2)}) copy-start(s32[1,16,12]{1,0,2:T(1,128)} %param.11) | copy-start | bytes 2308
  7.5 7.0 %copy-start = (bf16[1,256,4096]{2,1,0:T(8,128)(2,1)S(1)}, bf16[1,256,4096]{2,1,0:T(8,128)(2,1)}, u32[]{:S(2)}) copy-start(bf16[1,256,4096]{2,1,0:T(8,128)(2,1)} %param.7) | copy-start | bytes 6291460
  7.5 28.4 %collective-permute-start.5 = (bf16[256,4096]{1,0:T(8,128)(2,1)}, bf16[256,4096]{1,0:T(8,128)(2,1)}, u32[]{:S(2)}, u32[]{:S(2)}) collective-permute-start(bf16[256,4096]{1,0:T(8,128)(2,1)} %bitcast.79), channel_id=1, source_target_pairs={{12,28},{16,0},{13,29},{17,1},{14,30},{18,2},{15,31},{19,3}} | collective-permute-start | bytes 6291464 | tf_op jit(solution)/shard_map/ppermute | solution.py:144
  11.7 36.6 %collective-permute-start.7 = (bf16[256,2048]{1,0:T(8,128)(2,1)}, bf16[256,2048]{1,0:T(8,128)(2,1)}, u32[]{:S(2)}, u32[]{:S(2)}) collective-permute-start(bf16[256,2048]{1,0:T(8,128)(2,1)} %get-tuple-element.53), channel_id=1, source_target_pairs={{0,4},{4,8},{8,12},{16,20},{20,24},{24,28},{1,5},{5,9},{9,13},{17,... | collective-permute-start | bytes 3145736 | tf_op jit(solution)/shard_map/ppermute | solution.py:140
  14.5 1.6 copy-start.1
  14.5 5.5 %copy-start.13 = (f32[1024]{0:T(1024)S(1)}, f32[1024]{0:T(1024)}, u32[]{:S(2)}) copy-start(f32[1024]{0:T(1024)} %param.13) | copy-start | bytes 12292
  14.5 5.5 %copy-start.14 = (f32[1024]{0:T(1024)S(1)}, f32[1024]{0:T(1024)}, u32[]{:S(2)}) copy-start(f32[1024]{0:T(1024)} %param.12) | copy-start | bytes 12292
  18.7 34.9 %collective-permute-start.8 = (bf16[256,2048]{1,0:T(8,128)(2,1)}, bf16[256,2048]{1,0:T(8,128)(2,1)}, u32[]{:S(2)}, u32[]{:S(2)}) collective-permute-start(bf16[256,2048]{1,0:T(8,128)(2,1)} %get-tuple-element.53), channel_id=1, source_target_pairs={{4,0},{8,4},{12,8},{20,16},{24,20},{28,24},{5,1},{9,5},{13,9},{21,... | collective-permute-start | bytes 3145736 | tf_op jit(solution)/shard_map/ppermute | solution.py:141
  35.9 45.6 %collective-permute-start.6 = (bf16[256,4096]{1,0:T(8,128)(2,1)}, bf16[256,4096]{1,0:T(8,128)(2,1)}, u32[]{:S(2)}, u32[]{:S(2)}) collective-permute-start(bf16[256,4096]{1,0:T(8,128)(2,1)} %collective-permute-done.5), channel_id=1, source_target_pairs={{28,16},{0,12},{29,17},{1,13},{30,18},{2,14},{31,19},{3,15}} | collective-permute-start | bytes 6291464 | tf_op jit(solution)/shard_map/ppermute | solution.py:145
  40.7 2.0 copy-start.7
  42.7 9.6 %collective-permute-start.3 = (bf16[256,2048]{1,0:T(8,128)(2,1)}, bf16[256,2048]{1,0:T(8,128)(2,1)}, u32[]{:S(2)}, u32[]{:S(2)}) collective-permute-start(bf16[256,2048]{1,0:T(8,128)(2,1)} %get-tuple-element.55), channel_id=1, source_target_pairs={{0,4},{4,8},{8,12},{12,16},{16,20},{20,24},{24,28},{1,5},{5,9},{9,... | collective-permute-start | bytes 3145736 | tf_op jit(solution)/shard_map/ppermute | solution.py:135
  45.0 41.1 %collective-permute-start.4 = (bf16[256,2048]{1,0:T(8,128)(2,1)}, bf16[256,2048]{1,0:T(8,128)(2,1)}, u32[]{:S(2)}, u32[]{:S(2)}) collective-permute-start(bf16[256,2048]{1,0:T(8,128)(2,1)} %get-tuple-element.55), channel_id=1, source_target_pairs={{4,0},{8,4},{12,8},{16,12},{20,16},{24,20},{28,24},{5,1},{9,5},{13... | collective-permute-start | bytes 3145736 | tf_op jit(solution)/shard_map/ppermute | solution.py:136
  48.3 66.0 %collective-permute-start.11 = (bf16[256,2048]{1,0:T(8,128)(2,1)S(1)}, bf16[256,2048]{1,0:T(8,128)(2,1)}, u32[]{:S(2)}, u32[]{:S(2)}) collective-permute-start(bf16[256,2048]{1,0:T(8,128)(2,1)S(1)} %get-tuple-element.26), channel_id=1, source_target_pairs={{0,4},{4,8},{8,12},{16,20},{20,24},{24,28},{1,5},{5,9},{9,13},{17,... | collective-permute-start | bytes 3145736 | tf_op jit(solution)/shard_map/ppermute | solution.py:140
  52.3 63.2 %collective-permute-start.12 = (bf16[256,2048]{1,0:T(8,128)(2,1)S(1)}, bf16[256,2048]{1,0:T(8,128)(2,1)}, u32[]{:S(2)}, u32[]{:S(2)}) collective-permute-start(bf16[256,2048]{1,0:T(8,128)(2,1)S(1)} %get-tuple-element.26), channel_id=1, source_target_pairs={{4,0},{8,4},{12,8},{20,16},{24,20},{28,24},{5,1},{9,5},{13,9},{21,... | collective-permute-start | bytes 3145736 | tf_op jit(solution)/shard_map/ppermute | solution.py:141
  53.6 68.4 %collective-permute-start.9 = (bf16[256,2048]{1,0:T(8,128)(2,1)}, bf16[256,2048]{1,0:T(8,128)(2,1)}, u32[]{:S(2)}, u32[]{:S(2)}) collective-permute-start(bf16[256,2048]{1,0:T(8,128)(2,1)} %get-tuple-element.25), channel_id=1, source_target_pairs={{0,4},{4,8},{8,12},{12,16},{16,20},{20,24},{24,28},{1,5},{5,9},{9,... | collective-permute-start | bytes 3145736 | tf_op jit(solution)/shard_map/ppermute | solution.py:135
  81.5 40.5 %collective-permute-start.10 = (bf16[256,2048]{1,0:T(8,128)(2,1)}, bf16[256,2048]{1,0:T(8,128)(2,1)}, u32[]{:S(2)}, u32[]{:S(2)}) collective-permute-start(bf16[256,2048]{1,0:T(8,128)(2,1)} %get-tuple-element.25), channel_id=1, source_target_pairs={{4,0},{8,4},{12,8},{16,12},{20,16},{24,20},{28,24},{5,1},{9,5},{13... | collective-permute-start | bytes 3145736 | tf_op jit(solution)/shard_map/ppermute | solution.py:136
  108.5 64.3 %collective-permute-start.20 = (bf16[256,2048]{1,0:T(8,128)(2,1)}, bf16[256,2048]{1,0:T(8,128)(2,1)}, u32[]{:S(2)}, u32[]{:S(2)}) collective-permute-start(bf16[256,2048]{1,0:T(8,128)(2,1)} %get-tuple-element.35), channel_id=1, source_target_pairs={{0,4},{4,8},{8,12},{16,20},{20,24},{24,28},{1,5},{5,9},{9,13},{17,... | collective-permute-start | bytes 3145736 | tf_op jit(solution)/shard_map/ppermute | solution.py:140
  114.2 70.3 %collective-permute-start.19 = (bf16[256,2048]{1,0:T(8,128)(2,1)}, bf16[256,2048]{1,0:T(8,128)(2,1)}, u32[]{:S(2)}, u32[]{:S(2)}) collective-permute-start(bf16[256,2048]{1,0:T(8,128)(2,1)} %get-tuple-element.34), channel_id=1, source_target_pairs={{4,0},{8,4},{12,8},{20,16},{24,20},{28,24},{5,1},{9,5},{13,9},{21,... | collective-permute-start | bytes 3145736 | tf_op jit(solution)/shard_map/ppermute | solution.py:141
  117.1 34.1 %collective-permute-start.15 = (bf16[512,2048]{1,0:T(8,128)(2,1)}, bf16[512,2048]{1,0:T(8,128)(2,1)}, u32[]{:S(2)}, u32[]{:S(2)}) collective-permute-start(bf16[512,2048]{1,0:T(8,128)(2,1)} %pad_maximum_fusion.2), channel_id=1, source_target_pairs={{12,28},{16,0},{13,29},{17,1},{14,30},{18,2},{15,31},{19,3}} | collective-permute-start | bytes 6291464 | tf_op jit(solution)/shard_map/ppermute | solution.py:144
  122.0 28.4 %copy-start.9 = (bf16[256,2048]{1,0:T(8,128)(2,1)S(1)}, bf16[256,2048]{1,0:T(8,128)(2,1)}, u32[]{:S(2)}) copy-start(bf16[256,2048]{1,0:T(8,128)(2,1)} %get-tuple-element.24) | copy-start | bytes 3145732
  144.5 14.5 %collective-permute-start.18 = (bf16[256,2048]{1,0:T(8,128)(2,1)}, bf16[256,2048]{1,0:T(8,128)(2,1)}, u32[]{:S(2)}, u32[]{:S(2)}) collective-permute-start(bf16[256,2048]{1,0:T(8,128)(2,1)} %get-tuple-element.38), channel_id=1, source_target_pairs={{0,4},{4,8},{8,12},{12,16},{16,20},{20,24},{24,28},{1,5},{5,9},{9,... | collective-permute-start | bytes 3145736 | tf_op jit(solution)/shard_map/ppermute | solution.py:135
  149.0 1.7 copy-start.10
  149.0 17.7 %collective-permute-start.17 = (bf16[256,2048]{1,0:T(8,128)(2,1)}, bf16[256,2048]{1,0:T(8,128)(2,1)}, u32[]{:S(2)}, u32[]{:S(2)}) collective-permute-start(bf16[256,2048]{1,0:T(8,128)(2,1)} %get-tuple-element.37), channel_id=1, source_target_pairs={{4,0},{8,4},{12,8},{16,12},{20,16},{24,20},{28,24},{5,1},{9,5},{13... | collective-permute-start | bytes 3145736 | tf_op jit(solution)/shard_map/ppermute | solution.py:136
  151.3 45.7 %collective-permute-start.16 = (bf16[512,2048]{1,0:T(8,128)(2,1)}, bf16[512,2048]{1,0:T(8,128)(2,1)}, u32[]{:S(2)}, u32[]{:S(2)}) collective-permute-start(bf16[512,2048]{1,0:T(8,128)(2,1)} %collective-permute-done.15), channel_id=1, source_target_pairs={{28,16},{0,12},{29,17},{1,13},{30,18},{2,14},{31,19},{3,15}} | collective-permute-start | bytes 6291464 | tf_op jit(solution)/shard_map/ppermute | solution.py:145
  157.3 9.4 %copy-start.8 = (bf16[256,2048]{1,0:T(8,128)(2,1)S(1)}, bf16[256,2048]{1,0:T(8,128)(2,1)}, u32[]{:S(2)}) copy-start(bf16[256,2048]{1,0:T(8,128)(2,1)} %get-tuple-element.32) | copy-start | bytes 3145732
  159.0 26.8 %collective-permute-start.14 = (bf16[256,2048]{1,0:T(8,128)(2,1)}, bf16[256,2048]{1,0:T(8,128)(2,1)}, u32[]{:S(2)}, u32[]{:S(2)}) collective-permute-start(bf16[256,2048]{1,0:T(8,128)(2,1)} %get-tuple-element.33), channel_id=1, source_target_pairs={{0,4},{4,8},{8,12},{16,20},{20,24},{24,28},{1,5},{5,9},{9,13},{17,... | collective-permute-start | bytes 3145736 | tf_op jit(solution)/shard_map/ppermute | solution.py:140
  166.7 19.2 %collective-permute-start.13 = (bf16[256,2048]{1,0:T(8,128)(2,1)S(1)}, bf16[256,2048]{1,0:T(8,128)(2,1)}, u32[]{:S(2)}, u32[]{:S(2)}) collective-permute-start(bf16[256,2048]{1,0:T(8,128)(2,1)S(1)} %copy-done.8), channel_id=1, source_target_pairs={{4,0},{8,4},{12,8},{20,16},{24,20},{28,24},{5,1},{9,5},{13,9},{21,... | collective-permute-start | bytes 3145736 | tf_op jit(solution)/shard_map/ppermute | solution.py:141
  170.2 26.8 %copy-start.11 = (bf16[256,2048]{1,0:T(8,128)(2,1)S(1)}, bf16[256,2048]{1,0:T(8,128)(2,1)}, u32[]{:S(2)}) copy-start(bf16[256,2048]{1,0:T(8,128)(2,1)} %get-tuple-element.31) | copy-start | bytes 3145732
  170.2 26.8 %copy-start.12 = (bf16[256,2048]{1,0:T(8,128)(2,1)S(1)}, bf16[256,2048]{1,0:T(8,128)(2,1)}, u32[]{:S(2)}) copy-start(bf16[256,2048]{1,0:T(8,128)(2,1)} %get-tuple-element.39) | copy-start | bytes 3145732
  172.8 28.9 %copy-start.3 = (f32[256,2048]{1,0:T(8,128)}, f32[256,2048]{1,0:T(8,128)S(1)}, u32[]{:S(2)}) copy-start(f32[256,2048]{1,0:T(8,128)S(1)} %fusion.15) | copy-start | bytes 6291460
  172.8 34.7 %collective-permute-start.22 = (bf16[256,2048]{1,0:T(8,128)(2,1)}, bf16[256,2048]{1,0:T(8,128)(2,1)}, u32[]{:S(2)}, u32[]{:S(2)}) collective-permute-start(bf16[256,2048]{1,0:T(8,128)(2,1)} %get-tuple-element.42), channel_id=1, source_target_pairs={{0,4},{4,8},{8,12},{12,16},{16,20},{20,24},{24,28},{1,5},{5,9},{9,... | collective-permute-start | bytes 3145736 | tf_op jit(solution)/shard_map/ppermute | solution.py:135
  184.5 23.0 %collective-permute-start.21 = (bf16[256,2048]{1,0:T(8,128)(2,1)}, bf16[256,2048]{1,0:T(8,128)(2,1)}, u32[]{:S(2)}, u32[]{:S(2)}) collective-permute-start(bf16[256,2048]{1,0:T(8,128)(2,1)} %get-tuple-element.41), channel_id=1, source_target_pairs={{4,0},{8,4},{12,8},{16,12},{20,16},{24,20},{28,24},{5,1},{9,5},{13... | collective-permute-start | bytes 3145736 | tf_op jit(solution)/shard_map/ppermute | solution.py:136
  197.0 4.7 %copy-start.2 = (bf16[1,256,4096]{2,1,0:T(8,128)(2,1)S(1)}, bf16[1,256,4096]{2,1,0:T(8,128)(2,1)}, u32[]{:S(2)}) copy-start(bf16[1,256,4096]{2,1,0:T(8,128)(2,1)} %param.8) | copy-start | bytes 6291460
  201.7 1.7 copy-start.5
  203.5 6.6 %collective-permute-start.25 = (f32[2,1024]{1,0:T(2,128)S(1)}, f32[2,1024]{1,0:T(2,128)S(1)}, u32[]{:S(2)}, u32[]{:S(2)}) collective-permute-start(f32[2,1024]{1,0:T(2,128)S(1)} %bitcast.95), channel_id=1, source_target_pairs={{0,3},{1,0},{2,1},{3,2},{4,7},{5,4},{6,5},{7,6},{8,11},{9,8},{10,9... | collective-permute-start | bytes 24584 | tf_op jit(solution)/shard_map/ppermute | solution.py:117
  206.4 4.5 %collective-permute-start.24 = (f32[2,1024]{1,0:T(2,128)S(1)}, f32[2,1024]{1,0:T(2,128)S(1)}, u32[]{:S(2)}, u32[]{:S(2)}) collective-permute-start(f32[2,1024]{1,0:T(2,128)S(1)} %bitcast.96), channel_id=1, source_target_pairs={{0,2},{1,3},{2,0},{3,1},{4,6},{5,7},{6,4},{7,5},{8,10},{9,11},{10,... | collective-permute-start | bytes 24584 | tf_op jit(solution)/shard_map/ppermute | solution.py:117
  207.5 5.4 %collective-permute-start.23 = (f32[2,1024]{1,0:T(2,128)S(1)}, f32[2,1024]{1,0:T(2,128)S(1)}, u32[]{:S(2)}, u32[]{:S(2)}) collective-permute-start(f32[2,1024]{1,0:T(2,128)S(1)} %bitcast.97), channel_id=1, source_target_pairs={{0,1},{1,2},{2,3},{3,0},{4,5},{5,6},{6,7},{7,4},{8,9},{9,10},{10,1... | collective-permute-start | bytes 24584 | tf_op jit(solution)/shard_map/ppermute | solution.py:117
  207.5 9.6 %copy-start.4 = (f32[256,2048]{1,0:T(8,128)S(1)}, f32[256,2048]{1,0:T(8,128)}, u32[]{:S(2)}) copy-start(f32[256,2048]{1,0:T(8,128)} %copy-done.3) | copy-start | bytes 6291460
  207.5 9.6 %copy-start.6 = (f32[256,2048]{1,0:T(8,128)S(1)}, f32[256,2048]{1,0:T(8,128)}, u32[]{:S(2)}) copy-start(f32[256,2048]{1,0:T(8,128)} %copy-done.5) | copy-start | bytes 6291460
  212.9 4.1 %collective-permute-start.26 = (f32[2,1024]{1,0:T(2,128)S(1)}, f32[2,1024]{1,0:T(2,128)S(1)}, u32[]{:S(2)}, u32[]{:S(2)}) collective-permute-start(f32[2,1024]{1,0:T(2,128)S(1)} %fusion.17), channel_id=1, source_target_pairs={{0,4},{4,0},{8,12},{12,8},{16,20},{20,16},{24,28},{28,24},{1,5},{5... | collective-permute-start | bytes 24584 | tf_op jit(solution)/shard_map/ppermute | solution.py:123
  217.1 3.7 %collective-permute-start.27 = (f32[2,1024]{1,0:T(2,128)S(1)}, f32[2,1024]{1,0:T(2,128)S(1)}, u32[]{:S(2)}, u32[]{:S(2)}) collective-permute-start(f32[2,1024]{1,0:T(2,128)S(1)} %add.199), channel_id=1, source_target_pairs={{0,8},{4,12},{8,0},{12,4},{16,24},{20,28},{24,16},{28,20},{1,9},{5... | collective-permute-start | bytes 24584 | tf_op jit(solution)/shard_map/ppermute | solution.py:123
  220.7 3.7 %collective-permute-start.28 = (f32[2,1024]{1,0:T(2,128)S(1)}, f32[2,1024]{1,0:T(2,128)S(1)}, u32[]{:S(2)}, u32[]{:S(2)}) collective-permute-start(f32[2,1024]{1,0:T(2,128)S(1)} %add.200), channel_id=1, source_target_pairs={{0,16},{4,20},{8,24},{12,28},{16,0},{20,4},{24,8},{28,12},{1,17},{... | collective-permute-start | bytes 24584 | tf_op jit(solution)/shard_map/ppermute | solution.py:123
where the time goes:
time: 226 us; the launch traced here: 225 us
  starting transfers between devices  76.7 us (34%)
  waiting for transfers between devices  57.7 us (26%)
  Pallas kernels  44.8 us (20%)
  other arithmetic  37.9 us (17%)
  local copies, waits for them, and re-layouts  6.8 us (3%)
    pallas_call x2, Pallas kernels, attend(): pl.pallas_call(attend_kernel, grid=(steps,), in_specs=[fixed, whole, part...  44.8 us
    ppermute x2, waiting for transfers between devices, relay(): lax.ppermute(out, 'seq', [(frame_count - 1, middle), (0, middle - 1)])  35 us
    ppermute x4, starting transfers between devices, shards(): to_right = lambda x: lax.ppermute(x, 'seq', rightward)  22.6 us
    ppermute x4, starting transfers between devices, shards(): near_right = lambda x: lax.ppermute(x, 'seq', near(rightward))  18.3 us
    ppermute x2, waiting for transfers between devices, relay(): out = lax.ppermute(x, 'seq', [(middle - 1, frame_count - 1), (middle, 0)])  15.8 us
    ppermute x2, starting transfers between devices, relay(): lax.ppermute(out, 'seq', [(frame_count - 1, middle), (0, middle - 1)])  8.63 us
    convert_element_type x2, other arithmetic, shards(): sum((x.astype(jnp.float32) for x in terms)).astype(jnp.bfloat16)  7.17 us
    select_n x2, other arithmetic, shards(): vr = jnp.where(frame == middle - 1, far, vr)  6.76 us
  transfers between devices with their start and end apart: 29, of which 8 were waited for; matrix products, arithmetic and copies ran while one was open for 19% of the time, Pallas kernels for 20%

commit v1 on v0

--- a/solution.py
+++ b/solution.py
@@ -187,15 +187,15 @@
         )
         dq.append(dq_c.astype(jnp.float32))
         if c == 0:
-            far = relay(
-                jnp.concatenate(
-                    [jnp.where(frame == middle, dkl, dkr), jnp.where(frame == middle, dvl, dvr)]
-                ),
+            far = relay(jnp.where(frame == middle, dvl, dvr))
+            k_terms = (dko, to_left(dkl), to_right(dkr))
+            v_terms = (dvo, near_left(dvl), near_right(dvr), far)
+        else:
+            k_from_right, k_from_left = to_left(dkl), to_right(dkr)
+            k_terms = (dko, k_from_right, k_from_left)
+            dvl, dvr, k_from_right, k_from_left = lax.optimization_barrier(
+                (dvl, dvr, k_from_right, k_from_left)
             )
-            k_terms = (dko, near_left(dkl), near_right(dkr), far[:rows])
-            v_terms = (dvo, near_left(dvl), near_right(dvr), far[rows:])
-        else:
-            k_terms = (dko, to_left(dkl), to_right(dkr))
             v_terms = (dvo, to_left(dvl), to_right(dvr))
         wide = lambda terms: sum(x.astype(jnp.float32) for x in terms).astype(jnp.bfloat16)
         dk.append(wide(k_terms).astype(jnp.float32))

time: 226 us -> 227 us (level)
  waiting for transfers between devices: 57.7 us -> 61.6 us
  starting transfers between devices: 76.7 us -> 73 us
    ppermute x4 -> x5, starting transfers between devices: 22.6 us -> 14.5 us  [shards(): to_right = lambda x: lax.ppermute(x, 'seq', rightward)]
    ppermute x3, starting transfers between devices: 3.75 us -> 10.8 us  [sum_gains(): lax.ppermute(total, 'seq', [(i, i ^ step) for i in range(frame_count)])]
    ppermute x2, waiting for transfers between devices: 15.8 us -> 22.4 us  [relay(): out = lax.ppermute(x, 'seq', [(middle - 1, frame_count - 1), (middle, 0)])]
    convert_element_type x2, other arithmetic: 0.78 us -> 6.74 us  [shards(): dq.append(dq_c.astype(jnp.float32))]
    convert_element_type x2, other arithmetic: 7.17 us -> 1.24 us  [shards(): sum((x.astype(jnp.float32) for x in terms)).astype(jnp.bfloat16)]
    ppermute x2, waiting for transfers between devices: 35 us -> 37.9 us  [relay(): lax.ppermute(out, 'seq', [(frame_count - 1, middle), (0, middle - 1)])]
    ppermute x3, waiting for transfers between devices: 4.07 us -> 1.15 us  [sum_gains(): lax.ppermute(total, 'seq', [(i, i ^ step) for i in range(frame_count)])]
    ppermute x3, waiting for transfers between devices: 2.81 us -> 0.01 us  [sum_gains(): lax.ppermute(there, 'fsdp', [(i, (i + s) % count) for i in range(count)])]
  transfers between devices with their start and end apart: 29 -> 29, of which waited for: 8 -> 5; matrix products, arithmetic and copies ran while one was open for 19% -> 19% of each run, Pallas kernels for 20% -> 20%
where the time goes in v1:
time: 227 us; the launch traced here: 226 us
  starting transfers between devices  73 us (32%)
  waiting for transfers between devices  61.6 us (27%)
  Pallas kernels  44.8 us (20%)
  other arithmetic  40 us (18%)
  local copies, waits for them, and re-layouts  5.82 us (3%)
    pallas_call x2, Pallas kernels, attend(): pl.pallas_call(attend_kernel, grid=(steps,), in_specs=[fixed, whole, part...  44.8 us
    ppermute x2, waiting for transfers between devices, relay(): lax.ppermute(out, 'seq', [(frame_count - 1, middle), (0, middle - 1)])  37.9 us
    ppermute x2, waiting for transfers between devices, relay(): out = lax.ppermute(x, 'seq', [(middle - 1, frame_count - 1), (middle, 0)])  22.4 us
    ppermute x3, starting transfers between devices, shards(): near_right = lambda x: lax.ppermute(x, 'seq', near(rightward))  17.6 us
    ppermute x5, starting transfers between devices, shards(): to_right = lambda x: lax.ppermute(x, 'seq', rightward)  14.5 us
    ppermute x3, starting transfers between devices, sum_gains(): lax.ppermute(total, 'seq', [(i, i ^ step) for i in range(frame_count)])  10.8 us
    select_n x2, other arithmetic, shards(): vr = jnp.where(frame == middle - 1, far, vr)  6.76 us
    convert_element_type x2, other arithmetic, shards(): dq.append(dq_c.astype(jnp.float32))  6.74 us
  transfers between devices with their start and end apart: 29, of which 5 were waited for; matrix products, arithmetic and copies ran while one was open for 19% of the time, Pallas kernels for 20%

profile of v1, /device:TPU:0, one launch (start us, length us, event | category | flops | bytes accessed | tf_op | source)
XLA Modules:
  0.0 226.4 jit_solution(8515469959050515407)
XLA Ops:
  1.4 5.1 %collective-permute-start = (f32[2,1024]{1,0:T(2,128)S(1)}, f32[2,1024]{1,0:T(2,128)S(1)}, u32[]{:S(2)}, u32[]{:S(2)}) collective-permute-start(f32[2,1024]{1,0:T(2,128)S(1)} %pad_maximum_fusion.3), channel_id=1, source_target_pairs={{0,3},{1,0},{2,1},{3,2},{4,7},{5,4},{6,5},{7,6},{8,11},{9,8},{10,9... | collective-permute-start | bytes 24584 | tf_op jit(solution)/shard_map/ppermute | solution.py:99
  7.5 1.4 collective-permute-start.5
  8.9 2.7 %fusion.26 = (bf16[256,2048]{1,0:T(8,128)(2,1)}, bf16[256,2048]{1,0:T(8,128)(2,1)S(1)}) fusion(bf16[256,4096]{1,0:T(8,128)(2,1)} %bitcast.80), kind=kLoop, calls=%fused_computation.78 | loop fusion | bytes 4194304 | tf_op jit(solution)/shard_map/slice | solution.py:167
  11.6 2.8 %collective-permute-start.7 = (bf16[256,2048]{1,0:T(8,128)(2,1)}, bf16[256,2048]{1,0:T(8,128)(2,1)}, u32[]{:S(2)}, u32[]{:S(2)}) collective-permute-start(bf16[256,2048]{1,0:T(8,128)(2,1)} %get-tuple-element.55), channel_id=1, source_target_pairs={{0,4},{4,8},{8,12},{16,20},{20,24},{24,28},{1,5},{5,9},{9,13},{17,... | collective-permute-start | bytes 3145736 | tf_op jit(solution)/shard_map/ppermute | solution.py:140
  15.7 2.1 or_select_fusion.bias
  17.7 1.3 collective-permute-start.8
  19.2 16.7 %collective-permute-done.5 = bf16[256,4096]{1,0:T(8,128)(2,1)} collective-permute-done((bf16[256,4096]{1,0:T(8,128)(2,1)}, bf16[256,4096]{1,0:T(8,128)(2,1)}, u32[]{:S(2)}, u32[]{:S(2)}) %collective-permute-start.5) | collective-permute-done | bytes 2097184 | tf_op jit(solution)/shard_map/ppermute | solution.py:144
  35.9 2.6 %collective-permute-start.6 = (bf16[256,4096]{1,0:T(8,128)(2,1)}, bf16[256,4096]{1,0:T(8,128)(2,1)}, u32[]{:S(2)}, u32[]{:S(2)}) collective-permute-start(bf16[256,4096]{1,0:T(8,128)(2,1)} %collective-permute-done.5), channel_id=1, source_target_pairs={{28,16},{0,12},{29,17},{1,13},{30,18},{2,14},{31,19},{3,15}} | collective-permute-start | bytes 6291464 | tf_op jit(solution)/shard_map/ppermute | solution.py:145
  38.5 2.2 multiply_convert_fusion.ko
  40.7 1.6 fusion.27
  42.7 2.3 %collective-permute-start.3 = (bf16[256,2048]{1,0:T(8,128)(2,1)}, bf16[256,2048]{1,0:T(8,128)(2,1)}, u32[]{:S(2)}, u32[]{:S(2)}) collective-permute-start(bf16[256,2048]{1,0:T(8,128)(2,1)} %get-tuple-element.57), channel_id=1, source_target_pairs={{0,4},{4,8},{8,12},{12,16},{16,20},{20,24},{24,28},{1,5},{5,9},{9,... | collective-permute-start | bytes 3145736 | tf_op jit(solution)/shard_map/ppermute | solution.py:135
  45.0 1.3 collective-permute-start.4
  46.3 2.0 multiply_convert_fusion.1.q
  48.3 4.0 %collective-permute-start.11 = (bf16[256,2048]{1,0:T(8,128)(2,1)S(1)}, bf16[256,2048]{1,0:T(8,128)(2,1)}, u32[]{:S(2)}, u32[]{:S(2)}) collective-permute-start(bf16[256,2048]{1,0:T(8,128)(2,1)S(1)} %get-tuple-element.28), channel_id=1, source_target_pairs={{0,4},{4,8},{8,12},{16,20},{20,24},{24,28},{1,5},{5,9},{9,13},{17,... | collective-permute-start | bytes 3145736 | tf_op jit(solution)/shard_map/ppermute | solution.py:140
  52.3 1.3 collective-permute-start.12
  53.6 1.3 collective-permute-start.10
  54.9 24.8 %collective-permute-done.6 = bf16[256,4096]{1,0:T(8,128)(2,1)} collective-permute-done((bf16[256,4096]{1,0:T(8,128)(2,1)}, bf16[256,4096]{1,0:T(8,128)(2,1)}, u32[]{:S(2)}, u32[]{:S(2)}) %collective-permute-start.6) | collective-permute-done | bytes 2097184 | tf_op jit(solution)/shard_map/ppermute | solution.py:145
  79.7 2.4 %collective-permute-start.9 = (bf16[256,2048]{1,0:T(8,128)(2,1)}, bf16[256,2048]{1,0:T(8,128)(2,1)}, u32[]{:S(2)}, u32[]{:S(2)}) collective-permute-start(bf16[256,2048]{1,0:T(8,128)(2,1)} %get-tuple-element.27), channel_id=1, source_target_pairs={{0,4},{4,8},{8,12},{12,16},{16,20},{20,24},{24,28},{1,5},{5,9},{9,... | collective-permute-start | bytes 3145736 | tf_op jit(solution)/shard_map/ppermute | solution.py:135
  82.1 3.4 %broadcast_select_fusion.1 = (bf16[256,2048]{1,0:T(8,128)(2,1)}, bf16[256,2048]{1,0:T(8,128)(2,1)}) fusion(bf16[256,2048]{1,0:T(8,128)(2,1)} %collective-permute-done.8, pred[]{:T(512)S(6)} %eq.251, bf16[256,4096]{1,0:T(8,128)(2,1)} %collective-permute-done.6, bf16[256,2048]{1,0:T(8,128)(2,1)} %collective-permute-done.7, pred[]{:T(512)S(6)} %eq.250), kind=kLoop, calls=%fused_computation.36 | loop fusion | flops 1048576 | bytes 5242882 | tf_op jit(solution)/shard_map/jit(_where)/select_n | solution.py:184
  85.5 22.3 %shard_map.110 = (bf16[256,2048]{1,0:T(8,128)(2,1)}, bf16[256,2048]{1,0:T(8,128)(2,1)}, bf16[256,2048]{1,0:T(8,128)(2,1)}, bf16[256,2048]{1,0:T(8,128)(2,1)}, bf...) custom-call(f32[768,256]{1,0:T(8,128)} %or_select_fusion.bias, ...), custom_call_target="tpu_custom_call" | custom-call | flops 12079595520 | bytes 15728640 | tf_op jit(solution)/shard_map/pallas_call | solution.py:82
  107.8 1.3 collective-permute-start.13
  109.1 4.0 %collective-permute-start.14 = (bf16[256,2048]{1,0:T(8,128)(2,1)}, bf16[256,2048]{1,0:T(8,128)(2,1)}, u32[]{:S(2)}, u32[]{:S(2)}) collective-permute-start(bf16[256,2048]{1,0:T(8,128)(2,1)} %get-tuple-element.35), channel_id=1, source_target_pairs={{0,4},{4,8},{8,12},{12,16},{16,20},{20,24},{24,28},{1,5},{5,9},{9,... | collective-permute-start | bytes 3145736 | tf_op jit(solution)/shard_map/ppermute | solution.py:135
  113.2 3.8 %fusion.28 = (f32[256,2048]{1,0:T(8,128)}, f32[1,256,2048]{2,1,0:T(8,128)}) fusion(bf16[256,2048]{1,0:T(8,128)(2,1)} %get-tuple-element.26), kind=kLoop, calls=%fused_computation.80 | loop fusion | flops 524288 | bytes 5242880 | tf_op jit(solution)/shard_map/convert_element_type | solution.py:188
  116.9 3.4 %broadcast_select_fusion = (bf16[256,2048]{1,0:T(8,128)(2,1)}, bf16[256,2048]{1,0:T(8,128)(2,1)}) fusion(bf16[256,2048]{1,0:T(8,128)(2,1)} %collective-permute-done.12, pred[]{:T(512)S(6)} %eq.251, bf16[256,4096]{1,0:T(8,128)(2,1)} %collective-permute-done.6, bf16[256,2048]{1,0:T(8,128)(2,1)} %collective-permute-done.11, pred[]{:T(512)S(6)} %eq.250), kind=kLoop, calls=%fused_computation.35 | loop fusion | flops 1048576 | bytes 5242882 | tf_op jit(solution)/shard_map/jit(_where)/select_n | solution.py:184
  120.3 22.4 %shard_map.111 = (bf16[256,2048]{1,0:T(8,128)(2,1)}, bf16[256,2048]{1,0:T(8,128)(2,1)}, bf16[256,2048]{1,0:T(8,128)(2,1)}, bf16[256,2048]{1,0:T(8,128)(2,1)}, bf...) custom-call(f32[768,256]{1,0:T(8,128)} %or_select_fusion.bias, ...), custom_call_target="tpu_custom_call" | custom-call | flops 12079595520 | bytes 15728640 | tf_op jit(solution)/shard_map/pallas_call | solution.py:82
  142.8 1.3 collective-permute-start.15
  144.1 4.5 %collective-permute-start.16 = (bf16[256,2048]{1,0:T(8,128)(2,1)}, bf16[256,2048]{1,0:T(8,128)(2,1)}, u32[]{:S(2)}, u32[]{:S(2)}) collective-permute-start(bf16[256,2048]{1,0:T(8,128)(2,1)} %get-tuple-element.38), channel_id=1, source_target_pairs={{0,4},{4,8},{8,12},{12,16},{16,20},{20,24},{24,28},{1,5},{5,9},{9,... | collective-permute-start | bytes 3145736 | tf_op jit(solution)/shard_map/ppermute | solution.py:135
  148.6 3.0 %fusion.29 = (f32[256,2048]{1,0:T(8,128)S(1)}, f32[1,256,2048]{2,1,0:T(8,128)}) fusion(bf16[256,2048]{1,0:T(8,128)(2,1)} %get-tuple-element.32), kind=kLoop, calls=%fused_computation.81 | loop fusion | flops 524288 | bytes 5242880 | tf_op jit(solution)/shard_map/convert_element_type | solution.py:188
  151.6 1.7 multiply_reduce_fusion.1
  153.2 1.3 collective-permute-start.17
  154.6 2.5 %fusion.14 = f32[256,2048]{1,0:T(8,128)S(1)} fusion(bf16[256,2048]{1,0:T(8,128)(2,1)} %collective-permute-done.14, bf16[256,2048]{1,0:T(8,128)(2,1)} %collective-permute-done.13, bf16[256,2048]{1,0:T(8,128)(2,1)} %get-tuple-element.33), kind=kLoop, calls=%fused_computation.33 | loop fusion | flops 3670016 | bytes 5242880 | tf_op jit(solution)/shard_map/convert_element_type | solution.py:201
  157.1 2.8 %fusion.15 = f32[256,2048]{1,0:T(8,128)S(1)} fusion(bf16[256,2048]{1,0:T(8,128)(2,1)} %collective-permute-done.16, bf16[256,2048]{1,0:T(8,128)(2,1)} %collective-permute-done.15, bf16[256,2048]{1,0:T(8,128)(2,1)S(1)} %copy-done.12), kind=kLoop, calls=%fused_computation.34 | loop fusion | flops 3670016 | bytes 5242880 | tf_op jit(solution)/shard_map/convert_element_type | solution.py:201
  160.1 1.6 multiply_reduce_fusion
  161.8 2.5 %collective-permute-start.23 = (f32[2,1024]{1,0:T(2,128)S(1)}, f32[2,1024]{1,0:T(2,128)S(1)}, u32[]{:S(2)}, u32[]{:S(2)}) collective-permute-start(f32[2,1024]{1,0:T(2,128)S(1)} %bitcast.96), channel_id=1, source_target_pairs={{0,1},{1,2},{2,3},{3,0},{4,5},{5,6},{6,7},{7,4},{8,9},{9,10},{10,1... | collective-permute-start | bytes 24584 | tf_op jit(solution)/shard_map/ppermute | solution.py:117
  165.3 1.5 collective-permute-start.25
  166.8 1.3 broadcast_select_fusion.2
  168.1 10.9 %collective-permute-start.18 = (bf16[256,2048]{1,0:T(8,128)(2,1)S(1)}, bf16[256,2048]{1,0:T(8,128)(2,1)S(1)}, u32[]{:S(2)}, u32[]{:S(2)}) collective-permute-start(bf16[256,2048]{1,0:T(8,128)(2,1)S(1)} %copy-done.13), channel_id=1, source_target_pairs={{0,4},{4,8},{8,12},{16,20},{20,24},{24,28},{1,5},{5,9},{9,13},{17,... | collective-permute-start | bytes 3145736 | tf_op jit(solution)/shard_map/ppermute | solution.py:140
  179.0 1.3 collective-permute-start.19
  181.6 7.8 %collective-permute-start.27 = (f32[2,1024]{1,0:T(2,128)S(1)}, f32[2,1024]{1,0:T(2,128)S(1)}, u32[]{:S(2)}, u32[]{:S(2)}) collective-permute-start(f32[2,1024]{1,0:T(2,128)S(1)} %add.195), channel_id=1, source_target_pairs={{0,8},{4,12},{8,0},{12,4},{16,24},{20,28},{24,16},{28,20},{1,9},{5... | collective-permute-start | bytes 24584 | tf_op jit(solution)/shard_map/ppermute | solution.py:123
  189.4 3.5 %fusion.13 = bf16[1,256,4096]{2,1,0:T(8,128)(2,1)} fusion(bf16[1,256,4096]{2,1,0:T(8,128)(2,1)S(1)} %copy-done, f32[1,256,2048]{2,1,0:T(8,128)} %get-tuple-element.62, f32[1,256,2048]{2,1,0:T(8,128)S(1)} %copy-done.8, f32[256]{0:T(256)S(1)} %broadcast_multiply_fusion.1, f32[256]{0:T(256)S(1)} %add_sqrt_fusion.1, f32[4096]{0:T(1024)S(1)} %bitcast.88), kind=kLoop, calls=%fused_computation.27 | loop fusion | flops 8388608 | bytes 8407040 | tf_op jit(solution)/shard_map/convert_element_type | solution.py:27
  192.9 1.4 collective-permute-start.21
  194.4 2.9 %collective-permute-start.28 = (f32[2,1024]{1,0:T(2,128)S(1)}, f32[2,1024]{1,0:T(2,128)S(1)}, u32[]{:S(2)}, u32[]{:S(2)}) collective-permute-start(f32[2,1024]{1,0:T(2,128)S(1)} %add.196), channel_id=1, source_target_pairs={{0,16},{4,20},{8,24},{12,28},{16,0},{20,4},{24,8},{28,12},{1,17},{... | collective-permute-start | bytes 24584 | tf_op jit(solution)/shard_map/ppermute | solution.py:123
  197.3 5.7 %collective-permute-done.19 = bf16[256,2048]{1,0:T(8,128)(2,1)S(1)} collective-permute-done((bf16[256,2048]{1,0:T(8,128)(2,1)S(1)}, bf16[256,2048]{1,0:T(8,128)(2,1)S(1)}, u32[]{:S(2)}, u32[]{:S(2)}) %collective-permute-start.19) | collective-permute-done | bytes 1048608 | tf_op jit(solution)/shard_map/ppermute | solution.py:144
  203.0 1.3 collective-permute-start.22
  204.4 3.2 %collective-permute-start.20 = (bf16[256,2048]{1,0:T(8,128)(2,1)S(1)}, bf16[256,2048]{1,0:T(8,128)(2,1)S(1)}, u32[]{:S(2)}, u32[]{:S(2)}) collective-permute-start(bf16[256,2048]{1,0:T(8,128)(2,1)S(1)} %collective-permute-done.19), channel_id=1, source_target_pairs={{28,16},{0,12},{29,17},{1,13},{30,18},{2,14},{31,19},{3,15}} | collective-permute-start | bytes 3145736 | tf_op jit(solution)/shard_map/ppermute | solution.py:145
  207.7 2.2 fusion.12
  211.1 13.1 %collective-permute-done.20 = bf16[256,2048]{1,0:T(8,128)(2,1)S(1)} collective-permute-done((bf16[256,2048]{1,0:T(8,128)(2,1)S(1)}, bf16[256,2048]{1,0:T(8,128)(2,1)S(1)}, u32[]{:S(2)}, u32[]{:S(2)}) %collective-permute-start.20) | collective-permute-done | bytes 1048608 | tf_op jit(solution)/shard_map/ppermute | solution.py:145
  224.9 1.5 maximum_bitcast_fusion
  (99 shorter events, 7.8 us)
Async XLA Ops:
  1.4 16.4 %collective-permute-start = (f32[2,1024]{1,0:T(2,128)S(1)}, f32[2,1024]{1,0:T(2,128)S(1)}, u32[]{:S(2)}, u32[]{:S(2)}) collective-permute-start(f32[2,1024]{1,0:T(2,128)S(1)} %pad_maximum_fusion.3), channel_id=1, source_target_pairs={{0,3},{1,0},{2,1},{3,2},{4,7},{5,4},{6,5},{7,6},{8,11},{9,8},{10,9... | collective-permute-start | bytes 24584 | tf_op jit(solution)/shard_map/ppermute | solution.py:99
  6.5 12.6 %collective-permute-start.1 = (f32[2,1024]{1,0:T(2,128)S(1)}, f32[2,1024]{1,0:T(2,128)S(1)}, u32[]{:S(2)}, u32[]{:S(2)}) collective-permute-start(f32[2,1024]{1,0:T(2,128)S(1)} %pad_maximum_fusion.3), channel_id=1, source_target_pairs={{0,2},{1,3},{2,0},{3,1},{4,6},{5,7},{6,4},{7,5},{8,10},{9,11},{10,... | collective-permute-start | bytes 24584 | tf_op jit(solution)/shard_map/ppermute | solution.py:99
  6.5 12.6 %collective-permute-start.2 = (f32[2,1024]{1,0:T(2,128)S(1)}, f32[2,1024]{1,0:T(2,128)S(1)}, u32[]{:S(2)}, u32[]{:S(2)}) collective-permute-start(f32[2,1024]{1,0:T(2,128)S(1)} %pad_maximum_fusion.3), channel_id=1, source_target_pairs={{0,1},{1,2},{2,3},{3,0},{4,5},{5,6},{6,7},{7,4},{8,9},{9,10},{10,1... | collective-permute-start | bytes 24584 | tf_op jit(solution)/shard_map/ppermute | solution.py:99
  7.5 6.9 %copy-start.1 = (bf16[1,256,4096]{2,1,0:T(8,128)(2,1)S(1)}, bf16[1,256,4096]{2,1,0:T(8,128)(2,1)}, u32[]{:S(2)}) copy-start(bf16[1,256,4096]{2,1,0:T(8,128)(2,1)} %param.8) | copy-start | bytes 6291460
  7.5 28.4 %collective-permute-start.5 = (bf16[256,4096]{1,0:T(8,128)(2,1)}, bf16[256,4096]{1,0:T(8,128)(2,1)}, u32[]{:S(2)}, u32[]{:S(2)}) collective-permute-start(bf16[256,4096]{1,0:T(8,128)(2,1)} %bitcast.79), channel_id=1, source_target_pairs={{12,28},{16,0},{13,29},{17,1},{14,30},{18,2},{15,31},{19,3}} | collective-permute-start | bytes 6291464 | tf_op jit(solution)/shard_map/ppermute | solution.py:144
  11.6 3.3 %copy-start = (bf16[1,256,4096]{2,1,0:T(8,128)(2,1)S(1)}, bf16[1,256,4096]{2,1,0:T(8,128)(2,1)}, u32[]{:S(2)}) copy-start(bf16[1,256,4096]{2,1,0:T(8,128)(2,1)} %param.7) | copy-start | bytes 6291460
  11.6 36.6 %collective-permute-start.7 = (bf16[256,2048]{1,0:T(8,128)(2,1)}, bf16[256,2048]{1,0:T(8,128)(2,1)}, u32[]{:S(2)}, u32[]{:S(2)}) collective-permute-start(bf16[256,2048]{1,0:T(8,128)(2,1)} %get-tuple-element.55), channel_id=1, source_target_pairs={{0,4},{4,8},{8,12},{16,20},{20,24},{24,28},{1,5},{5,9},{9,13},{17,... | collective-permute-start | bytes 3145736 | tf_op jit(solution)/shard_map/ppermute | solution.py:140
  14.9 4.2 %copy-start.15 = (f32[1024]{0:T(1024)S(1)}, f32[1024]{0:T(1024)}, u32[]{:S(2)}) copy-start(f32[1024]{0:T(1024)} %param.13) | copy-start | bytes 12292
  14.9 4.2 %copy-start.16 = (f32[1024]{0:T(1024)S(1)}, f32[1024]{0:T(1024)}, u32[]{:S(2)}) copy-start(f32[1024]{0:T(1024)} %param.12) | copy-start | bytes 12292
  17.7 35.9 %collective-permute-start.8 = (bf16[256,2048]{1,0:T(8,128)(2,1)}, bf16[256,2048]{1,0:T(8,128)(2,1)}, u32[]{:S(2)}, u32[]{:S(2)}) collective-permute-start(bf16[256,2048]{1,0:T(8,128)(2,1)} %get-tuple-element.55), channel_id=1, source_target_pairs={{4,0},{8,4},{12,8},{20,16},{24,20},{28,24},{5,1},{9,5},{13,9},{21,... | collective-permute-start | bytes 3145736 | tf_op jit(solution)/shard_map/ppermute | solution.py:141
  35.9 43.9 %collective-permute-start.6 = (bf16[256,4096]{1,0:T(8,128)(2,1)}, bf16[256,4096]{1,0:T(8,128)(2,1)}, u32[]{:S(2)}, u32[]{:S(2)}) collective-permute-start(bf16[256,4096]{1,0:T(8,128)(2,1)} %collective-permute-done.5), channel_id=1, source_target_pairs={{28,16},{0,12},{29,17},{1,13},{30,18},{2,14},{31,19},{3,15}} | collective-permute-start | bytes 6291464 | tf_op jit(solution)/shard_map/ppermute | solution.py:145
  40.7 2.0 copy-start.9
  42.7 9.6 %collective-permute-start.3 = (bf16[256,2048]{1,0:T(8,128)(2,1)}, bf16[256,2048]{1,0:T(8,128)(2,1)}, u32[]{:S(2)}, u32[]{:S(2)}) collective-permute-start(bf16[256,2048]{1,0:T(8,128)(2,1)} %get-tuple-element.57), channel_id=1, source_target_pairs={{0,4},{4,8},{8,12},{12,16},{16,20},{20,24},{24,28},{1,5},{5,9},{9,... | collective-permute-start | bytes 3145736 | tf_op jit(solution)/shard_map/ppermute | solution.py:135
  45.0 40.5 %collective-permute-start.4 = (bf16[256,2048]{1,0:T(8,128)(2,1)}, bf16[256,2048]{1,0:T(8,128)(2,1)}, u32[]{:S(2)}, u32[]{:S(2)}) collective-permute-start(bf16[256,2048]{1,0:T(8,128)(2,1)} %get-tuple-element.57), channel_id=1, source_target_pairs={{4,0},{8,4},{12,8},{16,12},{20,16},{24,20},{28,24},{5,1},{9,5},{13... | collective-permute-start | bytes 3145736 | tf_op jit(solution)/shard_map/ppermute | solution.py:136
  48.3 60.9 %collective-permute-start.11 = (bf16[256,2048]{1,0:T(8,128)(2,1)S(1)}, bf16[256,2048]{1,0:T(8,128)(2,1)}, u32[]{:S(2)}, u32[]{:S(2)}) collective-permute-start(bf16[256,2048]{1,0:T(8,128)(2,1)S(1)} %get-tuple-element.28), channel_id=1, source_target_pairs={{0,4},{4,8},{8,12},{16,20},{20,24},{24,28},{1,5},{5,9},{9,13},{17,... | collective-permute-start | bytes 3145736 | tf_op jit(solution)/shard_map/ppermute | solution.py:140
  52.3 60.9 %collective-permute-start.12 = (bf16[256,2048]{1,0:T(8,128)(2,1)S(1)}, bf16[256,2048]{1,0:T(8,128)(2,1)}, u32[]{:S(2)}, u32[]{:S(2)}) collective-permute-start(bf16[256,2048]{1,0:T(8,128)(2,1)S(1)} %get-tuple-element.28), channel_id=1, source_target_pairs={{4,0},{8,4},{12,8},{20,16},{24,20},{28,24},{5,1},{9,5},{13,9},{21,... | collective-permute-start | bytes 3145736 | tf_op jit(solution)/shard_map/ppermute | solution.py:141
  53.6 66.7 %collective-permute-start.10 = (bf16[256,2048]{1,0:T(8,128)(2,1)}, bf16[256,2048]{1,0:T(8,128)(2,1)}, u32[]{:S(2)}, u32[]{:S(2)}) collective-permute-start(bf16[256,2048]{1,0:T(8,128)(2,1)} %get-tuple-element.27), channel_id=1, source_target_pairs={{4,0},{8,4},{12,8},{16,12},{20,16},{24,20},{28,24},{5,1},{9,5},{13... | collective-permute-start | bytes 3145736 | tf_op jit(solution)/shard_map/ppermute | solution.py:136
  79.7 40.6 %collective-permute-start.9 = (bf16[256,2048]{1,0:T(8,128)(2,1)}, bf16[256,2048]{1,0:T(8,128)(2,1)}, u32[]{:S(2)}, u32[]{:S(2)}) collective-permute-start(bf16[256,2048]{1,0:T(8,128)(2,1)} %get-tuple-element.27), channel_id=1, source_target_pairs={{0,4},{4,8},{8,12},{12,16},{16,20},{20,24},{24,28},{1,5},{5,9},{9,... | collective-permute-start | bytes 3145736 | tf_op jit(solution)/shard_map/ppermute | solution.py:135
  107.8 46.7 %collective-permute-start.13 = (bf16[256,2048]{1,0:T(8,128)(2,1)}, bf16[256,2048]{1,0:T(8,128)(2,1)}, u32[]{:S(2)}, u32[]{:S(2)}) collective-permute-start(bf16[256,2048]{1,0:T(8,128)(2,1)} %get-tuple-element.34), channel_id=1, source_target_pairs={{4,0},{8,4},{12,8},{16,12},{20,16},{24,20},{28,24},{5,1},{9,5},{13... | collective-permute-start | bytes 3145736 | tf_op jit(solution)/shard_map/ppermute | solution.py:136
  109.1 45.4 %collective-permute-start.14 = (bf16[256,2048]{1,0:T(8,128)(2,1)}, bf16[256,2048]{1,0:T(8,128)(2,1)}, u32[]{:S(2)}, u32[]{:S(2)}) collective-permute-start(bf16[256,2048]{1,0:T(8,128)(2,1)} %get-tuple-element.35), channel_id=1, source_target_pairs={{0,4},{4,8},{8,12},{12,16},{16,20},{20,24},{24,28},{1,5},{5,9},{9,... | collective-permute-start | bytes 3145736 | tf_op jit(solution)/shard_map/ppermute | solution.py:135
  142.8 14.3 %collective-permute-start.15 = (bf16[256,2048]{1,0:T(8,128)(2,1)}, bf16[256,2048]{1,0:T(8,128)(2,1)}, u32[]{:S(2)}, u32[]{:S(2)}) collective-permute-start(bf16[256,2048]{1,0:T(8,128)(2,1)} %get-tuple-element.37), channel_id=1, source_target_pairs={{4,0},{8,4},{12,8},{16,12},{20,16},{24,20},{28,24},{5,1},{9,5},{13... | collective-permute-start | bytes 3145736 | tf_op jit(solution)/shard_map/ppermute | solution.py:136
  144.1 13.0 %collective-permute-start.16 = (bf16[256,2048]{1,0:T(8,128)(2,1)}, bf16[256,2048]{1,0:T(8,128)(2,1)}, u32[]{:S(2)}, u32[]{:S(2)}) collective-permute-start(bf16[256,2048]{1,0:T(8,128)(2,1)} %get-tuple-element.38), channel_id=1, source_target_pairs={{0,4},{4,8},{8,12},{12,16},{16,20},{20,24},{24,28},{1,5},{5,9},{9,... | collective-permute-start | bytes 3145736 | tf_op jit(solution)/shard_map/ppermute | solution.py:135
  148.6 3.0 %copy-start.10 = (f32[256,2048]{1,0:T(8,128)S(1)}, f32[256,2048]{1,0:T(8,128)}, u32[]{:S(2)}) copy-start(f32[256,2048]{1,0:T(8,128)} %get-tuple-element.59) | copy-start | bytes 6291460
  153.2 57.8 %collective-permute-start.17 = (bf16[256,2048]{1,0:T(8,128)(2,1)}, bf16[256,2048]{1,0:T(8,128)(2,1)S(1)}, u32[]{:S(2)}, u32[]{:S(2)}) collective-permute-start(bf16[256,2048]{1,0:T(8,128)(2,1)} %get-tuple-element.40), channel_id=1, source_target_pairs={{4,0},{8,4},{12,8},{20,16},{24,20},{28,24},{5,1},{9,5},{13,9},{21,... | collective-permute-start | bytes 3145736 | tf_op jit(solution)/shard_map/ppermute | solution.py:141
  154.6 2.5 %copy-start.12 = (bf16[256,2048]{1,0:T(8,128)(2,1)S(1)}, bf16[256,2048]{1,0:T(8,128)(2,1)}, u32[]{:S(2)}) copy-start(bf16[256,2048]{1,0:T(8,128)(2,1)} %get-tuple-element.36) | copy-start | bytes 3145732
  157.1 2.9 %copy-start.4 = (f32[256,2048]{1,0:T(8,128)}, f32[256,2048]{1,0:T(8,128)S(1)}, u32[]{:S(2)}) copy-start(f32[256,2048]{1,0:T(8,128)S(1)} %fusion.14) | copy-start | bytes 6291460
  157.1 3.0 %copy-start.2 = (bf16[1,256,4096]{2,1,0:T(8,128)(2,1)S(1)}, bf16[1,256,4096]{2,1,0:T(8,128)(2,1)}, u32[]{:S(2)}) copy-start(bf16[1,256,4096]{2,1,0:T(8,128)(2,1)} %param.8) | copy-start | bytes 6291460
  160.1 1.6 copy-start.6
  161.7 6.4 %copy-start.13 = (bf16[256,2048]{1,0:T(8,128)(2,1)S(1)}, bf16[256,2048]{1,0:T(8,128)(2,1)}, u32[]{:S(2)}) copy-start(bf16[256,2048]{1,0:T(8,128)(2,1)} %get-tuple-element.41) | copy-start | bytes 3145732
  161.7 27.6 %copy-start.8 = (f32[1,256,2048]{2,1,0:T(8,128)S(1)}, f32[1,256,2048]{2,1,0:T(8,128)}, u32[]{:S(2)}) copy-start(f32[1,256,2048]{2,1,0:T(8,128)} %get-tuple-element.60) | copy-start | bytes 6291460
  161.8 17.2 %collective-permute-start.23 = (f32[2,1024]{1,0:T(2,128)S(1)}, f32[2,1024]{1,0:T(2,128)S(1)}, u32[]{:S(2)}, u32[]{:S(2)}) collective-permute-start(f32[2,1024]{1,0:T(2,128)S(1)} %bitcast.96), channel_id=1, source_target_pairs={{0,1},{1,2},{2,3},{3,0},{4,5},{5,6},{6,7},{7,4},{8,9},{9,10},{10,1... | collective-permute-start | bytes 24584 | tf_op jit(solution)/shard_map/ppermute | solution.py:117
  164.3 16.0 %collective-permute-start.24 = (f32[2,1024]{1,0:T(2,128)S(1)}, f32[2,1024]{1,0:T(2,128)S(1)}, u32[]{:S(2)}, u32[]{:S(2)}) collective-permute-start(f32[2,1024]{1,0:T(2,128)S(1)} %bitcast.95), channel_id=1, source_target_pairs={{0,2},{1,3},{2,0},{3,1},{4,6},{5,7},{6,4},{7,5},{8,10},{9,11},{10,... | collective-permute-start | bytes 24584 | tf_op jit(solution)/shard_map/ppermute | solution.py:117
  165.3 15.0 %collective-permute-start.25 = (f32[2,1024]{1,0:T(2,128)S(1)}, f32[2,1024]{1,0:T(2,128)S(1)}, u32[]{:S(2)}, u32[]{:S(2)}) collective-permute-start(f32[2,1024]{1,0:T(2,128)S(1)} %bitcast.97), channel_id=1, source_target_pairs={{0,3},{1,0},{2,1},{3,2},{4,7},{5,4},{6,5},{7,6},{8,11},{9,8},{10,9... | collective-permute-start | bytes 24584 | tf_op jit(solution)/shard_map/ppermute | solution.py:117
  168.1 42.9 %collective-permute-start.18 = (bf16[256,2048]{1,0:T(8,128)(2,1)S(1)}, bf16[256,2048]{1,0:T(8,128)(2,1)S(1)}, u32[]{:S(2)}, u32[]{:S(2)}) collective-permute-start(bf16[256,2048]{1,0:T(8,128)(2,1)S(1)} %copy-done.13), channel_id=1, source_target_pairs={{0,4},{4,8},{8,12},{16,20},{20,24},{24,28},{1,5},{5,9},{9,13},{17,... | collective-permute-start | bytes 3145736 | tf_op jit(solution)/shard_map/ppermute | solution.py:140
  179.0 24.0 %collective-permute-start.19 = (bf16[256,2048]{1,0:T(8,128)(2,1)S(1)}, bf16[256,2048]{1,0:T(8,128)(2,1)S(1)}, u32[]{:S(2)}, u32[]{:S(2)}) collective-permute-start(bf16[256,2048]{1,0:T(8,128)(2,1)S(1)} %broadcast_select_fusion.2), channel_id=1, source_target_pairs={{12,28},{16,0},{13,29},{17,1},{14,30},{18,2},{15,31},{19,3}} | collective-permute-start | bytes 3145736 | tf_op jit(solution)/shard_map/ppermute | solution.py:144
  180.4 1.2 collective-permute-start.26
  181.6 12.7 %collective-permute-start.27 = (f32[2,1024]{1,0:T(2,128)S(1)}, f32[2,1024]{1,0:T(2,128)S(1)}, u32[]{:S(2)}, u32[]{:S(2)}) collective-permute-start(f32[2,1024]{1,0:T(2,128)S(1)} %add.195), channel_id=1, source_target_pairs={{0,8},{4,12},{8,0},{12,4},{16,24},{20,28},{24,16},{28,20},{1,9},{5... | collective-permute-start | bytes 24584 | tf_op jit(solution)/shard_map/ppermute | solution.py:123
  189.4 3.6 %copy-start.19 = (bf16[256,2048]{1,0:T(8,128)(2,1)S(1)}, bf16[256,2048]{1,0:T(8,128)(2,1)}, u32[]{:S(2)}) copy-start(bf16[256,2048]{1,0:T(8,128)(2,1)} %get-tuple-element.45) | copy-start | bytes 3145732
  189.4 13.7 %copy-start.18 = (bf16[256,2048]{1,0:T(8,128)(2,1)S(1)}, bf16[256,2048]{1,0:T(8,128)(2,1)}, u32[]{:S(2)}) copy-start(bf16[256,2048]{1,0:T(8,128)(2,1)} %get-tuple-element.46) | copy-start | bytes 3145732
  189.4 18.3 %copy-start.3 = (bf16[1,256,4096]{2,1,0:T(8,128)(2,1)S(1)}, bf16[1,256,4096]{2,1,0:T(8,128)(2,1)}, u32[]{:S(2)}) copy-start(bf16[1,256,4096]{2,1,0:T(8,128)(2,1)} %param.8) | copy-start | bytes 6291460
  189.4 18.3 %copy-start.5 = (f32[256,2048]{1,0:T(8,128)S(1)}, f32[256,2048]{1,0:T(8,128)}, u32[]{:S(2)}) copy-start(f32[256,2048]{1,0:T(8,128)} %copy-done.4) | copy-start | bytes 6291460
  189.4 18.3 %copy-start.7 = (f32[256,2048]{1,0:T(8,128)S(1)}, f32[256,2048]{1,0:T(8,128)}, u32[]{:S(2)}) copy-start(f32[256,2048]{1,0:T(8,128)} %copy-done.6) | copy-start | bytes 6291460
  192.9 17.5 %collective-permute-start.21 = (bf16[256,2048]{1,0:T(8,128)(2,1)S(1)}, bf16[256,2048]{1,0:T(8,128)(2,1)S(1)}, u32[]{:S(2)}, u32[]{:S(2)}) collective-permute-start(bf16[256,2048]{1,0:T(8,128)(2,1)S(1)} %copy-done.19), channel_id=1, source_target_pairs={{4,0},{8,4},{12,8},{16,12},{20,16},{24,20},{28,24},{5,1},{9,5},{13... | collective-permute-start | bytes 3145736 | tf_op jit(solution)/shard_map/ppermute | solution.py:136
  194.4 10.0 %collective-permute-start.28 = (f32[2,1024]{1,0:T(2,128)S(1)}, f32[2,1024]{1,0:T(2,128)S(1)}, u32[]{:S(2)}, u32[]{:S(2)}) collective-permute-start(f32[2,1024]{1,0:T(2,128)S(1)} %add.196), channel_id=1, source_target_pairs={{0,16},{4,20},{8,24},{12,28},{16,0},{20,4},{24,8},{28,12},{1,17},{... | collective-permute-start | bytes 24584 | tf_op jit(solution)/shard_map/ppermute | solution.py:123
  203.0 7.4 %collective-permute-start.22 = (bf16[256,2048]{1,0:T(8,128)(2,1)S(1)}, bf16[256,2048]{1,0:T(8,128)(2,1)S(1)}, u32[]{:S(2)}, u32[]{:S(2)}) collective-permute-start(bf16[256,2048]{1,0:T(8,128)(2,1)S(1)} %copy-done.18), channel_id=1, source_target_pairs={{0,4},{4,8},{8,12},{12,16},{16,20},{20,24},{24,28},{1,5},{5,9},{9,... | collective-permute-start | bytes 3145736 | tf_op jit(solution)/shard_map/ppermute | solution.py:135
  204.4 19.8 %collective-permute-start.20 = (bf16[256,2048]{1,0:T(8,128)(2,1)S(1)}, bf16[256,2048]{1,0:T(8,128)(2,1)S(1)}, u32[]{:S(2)}, u32[]{:S(2)}) collective-permute-start(bf16[256,2048]{1,0:T(8,128)(2,1)S(1)} %collective-permute-done.19), channel_id=1, source_target_pairs={{28,16},{0,12},{29,17},{1,13},{30,18},{2,14},{31,19},{3,15}} | collective-permute-start | bytes 3145736 | tf_op jit(solution)/shard_map/ppermute | solution.py:145
  207.7 2.8 %copy-start.14 = (bf16[256,2048]{1,0:T(8,128)(2,1)S(1)}, bf16[256,2048]{1,0:T(8,128)(2,1)}, u32[]{:S(2)}) copy-start(bf16[256,2048]{1,0:T(8,128)(2,1)} %get-tuple-element.42) | copy-start | bytes 3145732
  210.5 13.7 %copy-start.11 = (bf16[256,2048]{1,0:T(8,128)(2,1)S(1)}, bf16[256,2048]{1,0:T(8,128)(2,1)}, u32[]{:S(2)}) copy-start(bf16[256,2048]{1,0:T(8,128)(2,1)} %get-tuple-element.39) | copy-start | bytes 3145732
  (1 other events, 1.0 us)
